TPU v7x, 32 devices: a whole 2x2x4 slice. The times are simulated.
32 devices in a mesh: elem: 8 (over y, x, core), mode: 4 (over z).
Axes of the slice: x: 2, y: 2, z: 4, core: 2. Of those that a mesh axis runs over, the one named last changes fastest.
Arguments:
- velocity: float32 [3, 5184, 2, 512], P(None, 'elem', None, 'mode'), may hold values from -3 to 3
- column_width: float32 [8], P('elem'), may hold values from 0.5 to 2
- row_height: float32 [8], replicated, may hold values from 0.5 to 2
- disc_mask: int32 [64], P('elem'), may hold values from 0 to 1, as said below
Outputs:
- velocity_new: float32 [3, 5184, 2, 512], P(None, 'elem', None, 'mode')
Inputs may be any that keep to these rules, and one draw needn't show every extreme that they name: `disc_mask`: in each column of 8 elements the ones form one run of 2 to 4 consecutive rows, counted cyclically in y.
All inputs are finite; a program needn't handle non-finite values.
Results may differ from a plain program's by a relative error of at most 0.0001.
Values sent between devices are 32-bit elements; how exact they have to be, the bound alone decides.
A program may use at most 128 MiB of HBM per device.

v0:
```python
import math
import jax
import jax.numpy as jnp
import numpy as np
from jax import lax
from jax.sharding import PartitionSpec as P

ORDER = 8
ITERS = 2
gll_points = [
    -1.0,
    -0.8997579954114602,
    -0.6771862795107377,
    -0.3631174638261782,
    0.0,
    0.3631174638261782,
    0.6771862795107377,
    0.8997579954114602,
    1.0,
]
gll_weights = [
    0.0277777777777778,
    0.1654953615608055,
    0.2745387125001617,
    0.3464285109730463,
    0.3715192743764172,
    0.3464285109730463,
    0.2745387125001617,
    0.1654953615608055,
    0.0277777777777778,
]
viscosity = 0.5
time_step = 0.02
thrust_coef = 4.0 / 3.0
highest = lax.Precision.HIGHEST


def padded(shard, sides, width):
    for axis, dim in sides:
        peers, length = (lax.axis_size(axis), shard.shape[dim])
        up = [(i, (i + 1) % peers) for i in range(peers)]
        down = [(j, i) for i, j in up]
        last = lax.slice_in_dim(shard, length - width, length, axis=dim)
        initial = lax.slice_in_dim(shard, 0, width, axis=dim)
        before = lax.ppermute(last, axis, up)
        after = lax.ppermute(initial, axis, down)
        shard = jnp.concatenate([before, shard, after], axis=dim)
    return shard


def node_tables():
    points = np.array(gll_points)
    identity = np.eye(9)
    differences = points[:, None] - points[None, :] + identity
    barycentric = 1.0 / np.prod(differences, axis=1)
    off_diagonal = barycentric[None, :] / barycentric[:, None] / differences * (1.0 - identity)
    derivative = off_diagonal - identity * off_diagonal.sum(axis=1)[:, None]
    return (
        jnp.asarray(derivative, dtype=jnp.float32),
        jnp.asarray(np.array(gll_weights), dtype=jnp.float32),
    )


def spectral_tables(mode_count):
    planes = 3 * mode_count
    wave_index = jnp.arange(mode_count, dtype=jnp.int32)
    plane_index = jnp.arange(planes, dtype=jnp.int32)
    phase_index = wave_index[:, None] * plane_index[None, :] % planes
    angles = 2.0 * math.pi / planes * phase_index.astype(jnp.float32)
    cosine_table = jnp.cos(angles)
    sine_table = jnp.sin(angles)
    mode_weight = jnp.where(wave_index == 0, 1.0, 2.0).astype(jnp.float32)[:, None] / math.sqrt(
        mode_count
    )
    wave_number = 8.0 / mode_count * wave_index.astype(jnp.float32)[:, None]
    inverse = jnp.concatenate([mode_weight * cosine_table, -mode_weight * sine_table], axis=0)
    spanwise = jnp.concatenate(
        [-wave_number * mode_weight * sine_table, -wave_number * mode_weight * cosine_table], axis=0
    )
    forward = (
        math.sqrt(mode_count) / planes * jnp.concatenate([cosine_table, -sine_table], axis=0).T
    )
    return (inverse, spanwise, forward)


def assemble(nodal_field):
    extended = padded(nodal_field, (("elem", 2),), 1)
    first_layer = nodal_field[:, :, 0] + extended[:, :, 0]
    last_layer = nodal_field[:, :, 8] + extended[:, :, 10]
    nodal_field = jnp.concatenate(
        [first_layer[:, :, None], nodal_field[:, :, 1:8], last_layer[:, :, None]], axis=2
    )
    upper_layer = nodal_field[:, :, :, 8] + jnp.roll(nodal_field[:, :, :, 0], -1, axis=1)
    return jnp.concatenate(
        [
            jnp.roll(upper_layer, 1, axis=1)[:, :, :, None],
            nodal_field[:, :, :, 1:8],
            upper_layer[:, :, :, None],
        ],
        axis=3,
    )


def apply_operator(nodal_field, derivative, quad_weights, ratio_x, ratio_y, jacobian, factor):
    grad_r = jnp.einsum("ij,pejbl->peibl", derivative, nodal_field, precision=highest)
    grad_s = jnp.einsum("ij,peajl->peail", derivative, nodal_field, precision=highest)
    flux_r = grad_r * quad_weights[None, None, :, :, None] * ratio_x[None, :, None, None, None]
    flux_s = grad_s * quad_weights[None, None, :, :, None] * ratio_y[None, :, None, None, None]
    stiffness = jnp.einsum("ji,pejbl->peibl", derivative, flux_r, precision=highest) + jnp.einsum(
        "ji,peajl->peail", derivative, flux_s, precision=highest
    )
    masses = (
        jacobian[None, :, None, None, None] * quad_weights[None, None, :, :, None] * nodal_field
    )
    return assemble(factor * masses + viscosity * stiffness)


def weighted_sum(left_field, right_field, multiplicity):
    return jnp.sum(left_field * right_field * multiplicity[None, None, :, :, None], axis=(1, 2, 3))


def paired(residual, image_field, multiplicity):
    return lax.psum(
        (
            weighted_sum(residual, residual, multiplicity),
            weighted_sum(residual, image_field, multiplicity),
        ),
        "elem",
    )


def on_device(velocity, column_width, row_height, disc_mask):
    derivative, weights = node_tables()
    quad_weights = weights[:, None] * weights[None, :]
    node_index = jnp.arange(9)
    edge_count = jnp.where((node_index == 0) | (node_index == 8), 2.0, 1.0).astype(jnp.float32)
    multiplicity = 1.0 / (edge_count[:, None] * edge_count[None, :])
    groups = lax.axis_size("mode")
    local_modes = velocity.shape[3]
    mode_count = groups * local_modes
    planes = 3 * mode_count
    elements = velocity.shape[1] // 81
    local_elems = elements // groups
    col_width = column_width[0]
    inverse, spanwise, forward = spectral_tables(mode_count)
    nodal_field = velocity.reshape(3, elements, 9, 9, 2 * local_modes)
    mode_index = lax.axis_index("mode") * local_modes + jnp.arange(local_modes, dtype=jnp.int32)
    wavenumber = 8.0 / mode_count * mode_index.astype(jnp.float32)
    elem_start = lax.axis_index("mode") * local_elems
    local_heights = lax.dynamic_slice_in_dim(row_height, elem_start, local_elems)
    local_disc = lax.dynamic_slice_in_dim(disc_mask, elem_start, local_elems).astype(jnp.float32)
    members = lax.all_to_all(velocity, "mode", split_axis=1, concat_axis=3, tiled=True)
    flat_items = members.reshape(members.shape[0], members.shape[1], 2 * mode_count)
    values = jnp.einsum("pnl,lq->pnq", flat_items, inverse, precision=highest)
    along_z = jnp.einsum("pnl,lq->pnq", flat_items, spanwise, precision=highest)
    values = values.reshape(3, local_elems, 9, 9, planes)
    along_z = along_z.reshape(3, local_elems, 9, 9, planes)
    along_x = 2.0 / col_width * jnp.einsum("ij,pejbq->peibq", derivative, values, precision=highest)
    along_y = (2.0 / local_heights)[None, :, None, None, None] * jnp.einsum(
        "ij,peajq->peaiq", derivative, values, precision=highest
    )
    advection = values[0][None] * along_x + values[1][None] * along_y + values[2][None] * along_z
    plane_index = jnp.arange(planes)
    in_disc = ((plane_index >= 3 * planes // 8) & (plane_index < 5 * planes // 8)).astype(
        jnp.float32
    )
    disc_planes = 5 * planes // 8 - 3 * planes // 8
    local_jacobian = col_width * local_heights / 4.0
    node_weight = (local_disc * local_jacobian)[:, None, None] * quad_weights[None]
    partial_total = jnp.sum(node_weight[:, :, :, None] * values[0] * values[0] * in_disc)
    disc_total = lax.psum(partial_total, "mode")
    disc_area = disc_planes * col_width * jnp.sum(disc_mask.astype(jnp.float32) * row_height)
    pressure = disc_total / disc_area
    thrust = (
        -(0.5 * thrust_coef * ORDER)
        * pressure
        / col_width
        * local_disc[:, None, None, None]
        * in_disc
    )
    tendency = jnp.concatenate([(thrust - advection[0])[None], -advection[1:]], axis=0)
    spectral = jnp.einsum("peabq,ql->peabl", tendency, forward, precision=highest)
    spectral = spectral.reshape(3, local_elems * 81, 2, mode_count)
    returned = lax.all_to_all(spectral, "mode", split_axis=3, concat_axis=1, tiled=True)
    u_star = nodal_field + time_step * returned.reshape(3, elements, 9, 9, 2 * local_modes)
    jacobian = col_width * row_height / 4.0
    ratio_x = row_height / col_width
    ratio_y = col_width / row_height
    single = 1.0 / time_step + viscosity * wavenumber * wavenumber
    factor = jnp.concatenate([single, single])
    right_side = (
        assemble(
            jacobian[None, :, None, None, None] * quad_weights[None, None, :, :, None] * u_star
        )
        / time_step
    )
    residual = right_side
    solution = jnp.zeros_like(right_side)
    image_field = apply_operator(
        residual, derivative, quad_weights, ratio_x, ratio_y, jacobian, factor
    )
    norm_now, product = paired(residual, image_field, multiplicity)
    step_size = norm_now / product
    direction = residual
    along_image = image_field
    for iteration in range(ITERS):
        solution = solution + step_size[:, None, None, None, :] * direction
        residual = residual - step_size[:, None, None, None, :] * along_image
        if iteration + 1 < ITERS:
            image_field = apply_operator(
                residual, derivative, quad_weights, ratio_x, ratio_y, jacobian, factor
            )
            norm_next, product = paired(residual, image_field, multiplicity)
            beta_ratio = norm_next / norm_now
            step_size = norm_next / (product - beta_ratio * norm_next / step_size)
            direction = residual + beta_ratio[:, None, None, None, :] * direction
            along_image = image_field + beta_ratio[:, None, None, None, :] * along_image
            norm_now = norm_next
    return solution.reshape(3, elements * 81, 2, local_modes)


def solution(mesh):
    return jax.shard_map(
        on_device,
        mesh=mesh,
        in_specs=(P(None, "elem", None, "mode"), P("elem"), P(), P("elem")),
        out_specs=P(None, "elem", None, "mode"),
        check_vma=False,
    )
```

profile of v0, /device:TPU:0, one launch (start us, length us, event | category | flops | bytes accessed | tf_op | source)
XLA Modules:
  0.0 403.9 jit_solution(6718678095885858187)
XLA Ops:
  3.6 6.3 %all-to-all-start = ((f32[3,648,2,128]{3,2,0,1:T(2,128)}), f32[3,648,2,128]{3,2,0,1:T(2,128)S(1)}, u32[]{:S(2)}, u32[]{:S(2)}) async-start(f32[3,648,2,128]{3,2,0,1:T(2,128)} %copy.119), calls=%async_computation | async-start | bytes 3981312 | tf_op jit(solution)/shard_map/all_to_all | solution.py:152
  13.6 14.0 %fusion.61 = (f32[512,1536]{1,0:T(8,128)}, f32[512,1536]{1,0:T(8,128)}) fusion(), kind=kLoop, calls=%fused_computation.87 | loop fusion | flops 7864320 | bytes 6291456 | tf_op jit(solution)/shard_map/cos | solution.py:70
  27.5 14.2 %fusion.63 = (f32[512,1536]{1,0:T(8,128)}, f32[512,1536]{1,0:T(8,128)}) fusion(f32[512]{0:T(512)S(1)} %negate_multiply_fusion), kind=kLoop, calls=%fused_computation.89 | loop fusion | flops 8650752 | bytes 6293504 | tf_op jit(solution)/shard_map/mul | solution.py:78
  41.7 14.2 %fusion.64 = (f32[512,1536]{1,0:T(8,128)}, f32[512,1536]{1,0:T(8,128)}) fusion(f32[512]{0:T(512)S(1)} %fusion.77, f32[512]{0:T(512)S(1)} %select_multiply_fusion), kind=kLoop, calls=%fused_computation.90 | loop fusion | flops 8650752 | bytes 6295552 | tf_op jit(solution)/shard_map/mul | solution.py:76
  61.3 13.4 %fusion.54 = f32[3,162,1536]{2,1,0:T(8,128)S(1)} fusion(f32[3,162,1024]{2,1,0:T(8,128)} %reshape.205, f32[512,1536]{1,0:T(8,128)S(1)} %copy-done.11, f32[512,1536]{1,0:T(8,128)} %get-tuple-element.64), kind=kOutput, calls=%fused_computation.79 | convolution fusion | flops 9174515712 | bytes 11268096 | tf_op jit(solution)/shard_map/pnl,lq->pnq/dot_general | solution.py:154
  92.9 13.4 %fusion.53 = f32[3,162,1536]{2,1,0:T(8,128)S(1)} fusion(f32[3,162,1024]{2,1,0:T(8,128)} %reshape.205, f32[512,1536]{1,0:T(8,128)} %get-tuple-element.56, f32[512,1536]{1,0:T(8,128)S(1)} %copy-done.10), kind=kOutput, calls=%fused_computation.78 | convolution fusion | flops 9174515712 | bytes 11268096 | tf_op jit(solution)/shard_map/pnl,lq->pnq/dot_general | solution.py:155
  110.6 12.8 %psum.35 = f32[]{:T(128)} all-reduce(f32[]{:T(128)} %get-tuple-element.35), channel_id=1, replica_groups=mesh['elem'=8,'mode'=4] {'mode'}, use_global_device_ids=true, to_apply=%region_1.2 | all-reduce | flops 1 | bytes 8 | tf_op jit(solution)/shard_map/psum | solution.py:171
  125.6 11.5 %fusion.16 = f32[3,2,9,1536,9]{3,4,2,1,0:T(8,128)} fusion(f32[9,9,1,1,1]{1,0,4,3,2:T(8,128)S(1)} %copy-done.13, f32[3,2,9,9,1536]{4,0,3,2,1:T(4,128)} %bitcast.137), kind=kOutput, calls=%fused_computation.24 | convolution fusion | flops 80621568 | bytes 5972292 | tf_op jit(solution)/shard_map/ij,peajq->peaiq/dot_general | solution.py:159
  137.1 14.2 %fusion.15 = f32[3,2,9,9,1536]{4,2,3,1,0:T(8,128)S(1)} fusion(f32[3,2,9,9,1536]{4,0,3,2,1:T(4,128)S(1)} %bitcast.139, f32[3,2,9,1536,9]{3,4,2,1,0:T(8,128)} %fusion.16, f32[9,9,1,1,1]{1,0,4,3,2:T(8,128)S(1)} %copy-done.13, f32[3,2,9,9,1536]{4,0,3,2,1:T(4,128)S(1)} %bitcast.138, f32[2,9,9,1536]{3,1,2,0:T(8,128)S(1)} %copy-done.3, f32[2]{0:T(128)S(1)} %copy-done.30, ...), kind=kOutput, calls=%fused_computation.20 | convolution fusion | flops 85847040 | bytes 14930256 | tf_op jit(solution)/shard_map/ij,pejbq->peibq/dot_general | solution.py:158
  154.3 17.1 %fusion.7 = f32[3,2,9,9,1024]{4,2,3,1,0:T(8,128)S(1)} fusion(f32[512,1536]{1,0:T(8,128)S(1)} %copy-done.9, f32[512,1536]{1,0:T(8,128)S(1)} %copy-done.8, f32[2,2,9,9,1536]{4,2,3,1,0:T(8,128)S(1)} %slice_negate_fusion, f32[1,2,9,9,1536]{4,2,3,1,0:T(8,128)S(1)} %slice_subtract_fusion), kind=kOutput, calls=%fused_computation.10 | convolution fusion | flops 9176835072 | bytes 11268096 | tf_op jit(solution)/shard_map/peabq,ql->peabl/dot_general | solution.py:182
  176.0 6.6 %copy.132 = f32[3,162,2,512]{1,2,0,3:T(2,128)} copy(f32[3,162,2,512]{3,2,0,1:T(2,128)} %reshape.208) | data formatting | bytes 3981312 | tf_op jit(solution)/shard_map/reshape | solution.py:183
  192.3 63.4 %all-to-all-done.1 = f32[3,162,2,512]{1,2,0,3:T(2,128)} async-done(((f32[3,162,2,512]{1,2,0,3:T(2,128)}), f32[3,162,2,512]{1,2,0,3:T(2,128)}, u32[]{:S(2)}, u32[]{:S(2)}) %all-to-all-start.1) | async-done | bytes 1990688 | tf_op jit(solution)/shard_map/all_to_all | solution.py:184
  255.6 5.2 %broadcast_multiply_fusion = f32[3,162,2,512]{1,2,0,3:T(2,128)} fusion(f32[3,162,2,512]{1,2,0,3:T(2,128)} %all-to-all-done.1), kind=kLoop, calls=%fused_computation.101 | loop fusion | flops 497664 | bytes 3981312 | tf_op jit(solution)/shard_map/mul | solution.py:185
  260.8 6.4 %copy.133 = f32[3,162,2,4,128]{4,2,0,1,3:T(2,128)} copy(f32[3,162,2,4,128]{1,2,0,4,3:T(2,128)} %bitcast.140) | data formatting | bytes 3981312 | tf_op jit(solution)/shard_map/mul | solution.py:185
  267.2 4.7 %mul.655 = f32[3,8,9,9,256]{4,0,3,2,1:T(4,128)} reshape(f32[3,4,162,2,128]{4,3,0,2,1:T(2,128)} %bitcast.143) | data formatting | bytes 3981312 | tf_op jit(solution)/shard_map/mul | solution.py:185
  285.0 4.9 %fusion.44 = f32[3,8,9,256,9]{3,4,2,1,0:T(8,128)S(1)} fusion(f32[9,9,1,1,1]{1,0,4,3,2:T(8,128)S(1)} %copy-done.13, f32[3,8,9,9,256]{4,2,3,1,0:T(8,128)S(1)} %copy_multiply_fusion.4), kind=kOutput, calls=%fused_computation.64 | convolution fusion | flops 53747712 | bytes 3981636 | tf_op jit(solution)/shard_map/ij,peajl->peail/dot_general | solution.py:106
  298.2 5.9 %fusion.32 = f32[3,8,9,9,256]{4,2,0,1,3:T(8,128)S(1)} fusion(f32[3,8,9,256,9]{3,4,2,1,0:T(8,128)S(1)} %fusion.33, f32[8,9,9]{1,0,2:T(8,128)S(1)} %copy-done.22, f32[256]{0:T(256)S(1)} %pad_maximum_fusion.6, f32[3,8,9,1,256]{4,2,0,1,3:T(8,128)S(1)} %maximum_add_fusion.1, f32[3,8,1,9,256]{4,2,0,1,3:T(1,128)S(1)} %get-tuple-element.32, ...), kind=kOutput, calls=%fused_computation.48 | convolution fusion | flops 61212672 | bytes 8408932 | tf_op jit(solution)/shard_map/ji,pejbl->peibl/dot_general | solution.py:109
  316.5 14.7 %all-reduce.1 = (f32[3,256]{1,0:T(4,128)}, f32[3,256]{1,0:T(4,128)}) all-reduce(f32[3,256]{1,0:T(4,128)} %get-tuple-element.8, f32[3,256]{1,0:T(4,128)} %get-tuple-element.7), channel_id=1, replica_groups=mesh['elem'=8,'mode'=4] {'elem'}, use_global_device_ids=true, to_apply=%region_4.5 | all-reduce | flops 1536 | bytes 12288 | tf_op jit(solution)/shard_map/psum | solution.py:123
  332.5 5.0 %multiply_subtract_fusion = (f32[3,8,9,9,256]{4,2,3,1,0:T(8,128)S(1)}, f32[3,8,9,9,256]{4,2,3,1,0:T(8,128)}) fusion(f32[3,256]{1,0:T(4,128)S(1)} %get-tuple-element.14, f32[3,8,9,9,256]{4,2,0,1,3:T(8,128)S(1)} %fusion.25, f32[3,8,9,1,256]{4,2,3,1,0:T(8,128)} %copy-done.7, f32[3,7,9,256]{3,2,0,1:T(8,128)} %copy-done.12, f32[3,1,9,256]{3,2,0,1:T(8,128)} %copy-done.14, ...), kind=kLoop, calls=%fused_computation.72 | loop fusion | flops 2543616 | bytes 7965696 | tf_op jit(solution)/shard_map/sub | solution.py:208
  337.5 4.9 %fusion.39 = f32[3,8,9,256,9]{3,4,2,1,0:T(8,128)S(1)} fusion(f32[9,9,1,1,1]{1,0,4,3,2:T(8,128)S(1)} %copy-done.13, f32[3,8,9,9,256]{4,2,3,1,0:T(8,128)S(1)} %get-tuple-element.25), kind=kOutput, calls=%fused_computation.58 | convolution fusion | flops 53747712 | bytes 3981636 | tf_op jit(solution)/shard_map/ij,peajl->peail/dot_general | solution.py:106
  350.0 5.2 %fusion.27 = f32[3,8,9,9,256]{4,2,0,1,3:T(8,128)S(1)} fusion(f32[3,8,9,256,9]{3,4,2,1,0:T(8,128)S(1)} %fusion.28, f32[3,8,9,9,256]{4,2,3,1,0:T(8,128)S(1)} %get-tuple-element.25, f32[9,9,1,1,1]{1,0,2,3,4:T(8,128)S(1)} %copy-done.29, f32[3,8,9,9,256]{4,2,3,1,0:T(8,128)S(1)} %fusion.30, f32[256]{0:T(256)S(1)} %copy-done.40, f32[8,9,9]{1,0,2:T(8,128)S(1)} %copy-done.15), kind=kOutput, calls=%fused_computation.41 | convolution fusion | flops 56236032 | bytes 7966564 | tf_op jit(solution)/shard_map/ji,pejbl->peibl/dot_general | solution.py:109
  363.8 4.8 %concatenate.89 = f32[3,648,2,128]{3,2,0,1:T(2,128)} reshape(f32[3,8,9,9,256]{4,0,3,2,1:T(4,128)} %copy.136) | data formatting | bytes 3981312 | tf_op jit(solution)/shard_map/concatenate | solution.py:94
  370.3 5.0 %copy.155 = f32[3,8,9,9,256]{4,0,3,2,1:T(4,128)} copy(f32[3,8,9,9,256]{4,2,3,1,0:T(8,128)} %get-tuple-element.26) | data formatting | bytes 3981312 | tf_op jit(solution)/shard_map/concatenate | solution.py:94
  385.7 12.0 %all-reduce = (f32[3,256]{1,0:T(4,128)S(1)}, f32[3,256]{1,0:T(4,128)S(1)}) all-reduce(f32[3,256]{1,0:T(4,128)S(1)} %get-tuple-element.6, f32[3,256]{1,0:T(4,128)S(1)} %get-tuple-element.5), channel_id=1, replica_groups=mesh['elem'=8,'mode'=4] {'elem'}, use_global_device_ids=true, to_apply=%region_8.9 | all-reduce | flops 1536 | bytes 12288 | tf_op jit(solution)/shard_map/psum | solution.py:123
  (182 shorter events, 120.6 us)
Async XLA Ops:
  0.0 10.6 %copy-start.37 = (f32[9]{0:T(128)S(1)}, f32[9]{0:T(128)}, u32[]{:S(2)}) copy-start(f32[9]{0:T(128)} %constant.72.clone) | copy-start | bytes 112
  0.0 10.7 %copy-start.38 = (f32[8]{0:T(128)S(1)}, f32[8]{0:T(128)}, u32[]{:S(2)}) copy-start(f32[8]{0:T(128)} %param.8) | copy-start | bytes 100
  0.0 10.7 %copy-start.35 = (s32[8]{0:T(128)S(1)}, s32[8]{0:T(128)}, u32[]{:S(2)}) copy-start(s32[8]{0:T(128)} %param.9) | copy-start | bytes 100
  3.6 52.3 %all-to-all-start = ((f32[3,648,2,128]{3,2,0,1:T(2,128)}), f32[3,648,2,128]{3,2,0,1:T(2,128)S(1)}, u32[]{:S(2)}, u32[]{:S(2)}) async-start(f32[3,648,2,128]{3,2,0,1:T(2,128)} %copy.119), calls=%async_computation | async-start | bytes 3981312 | tf_op jit(solution)/shard_map/all_to_all | solution.py:152
  10.7 31.0 %copy-start.16 = (f32[9,9]{1,0:T(8,128)}, f32[9,9]{1,0:T(8,128)S(1)}, u32[]{:S(2)}) copy-start(f32[9,9]{1,0:T(8,128)S(1)} %copy.118) | copy-start | bytes 976
  13.6 65.5 %copy-start.21 = (f32[1536]{0:T(1024)}, f32[1536]{0:T(1024)S(1)}, u32[]{:S(2)}) copy-start(f32[1536]{0:T(1024)S(1)} %fusion.76) | copy-start | bytes 18436
  106.3 19.2 %copy-start.13 = (f32[9,9,1,1,1]{1,0,4,3,2:T(8,128)S(1)}, f32[9,9,1,1,1]{1,0,4,3,2:T(8,128)}, u32[]{:S(2)}) copy-start(f32[9,9,1,1,1]{1,0,4,3,2:T(8,128)} %constant.74) | copy-start | bytes 976
  125.6 11.5 %copy-start.2 = (f32[3,162,1536]{2,0,1:T(4,128)S(1)}, f32[3,162,1536]{2,0,1:T(4,128)}, u32[]{:S(2)}) copy-start(f32[3,162,1536]{2,0,1:T(4,128)} %copy.122) | copy-start | bytes 8957956
  125.6 11.5 %copy-start.3 = (f32[2,9,9,1536]{3,1,2,0:T(8,128)S(1)}, f32[2,9,9,1536]{3,1,2,0:T(8,128)}, u32[]{:S(2)}) copy-start(f32[2,9,9,1536]{3,1,2,0:T(8,128)} %copy.127) | copy-start | bytes 2985988
  125.6 11.5 %copy-start.5 = (f32[3,162,1536]{2,0,1:T(4,128)S(1)}, f32[3,162,1536]{2,0,1:T(4,128)}, u32[]{:S(2)}) copy-start(f32[3,162,1536]{2,0,1:T(4,128)} %copy.128) | copy-start | bytes 8957956
  125.6 11.5 %copy-start.30 = (f32[2]{0:T(128)S(1)}, f32[2]{0:T(128)}, u32[]{:S(2)}) copy-start(f32[2]{0:T(128)} %get-tuple-element.62) | copy-start | bytes 28
  182.5 73.1 %all-to-all-start.1 = ((f32[3,162,2,512]{1,2,0,3:T(2,128)}), f32[3,162,2,512]{1,2,0,3:T(2,128)}, u32[]{:S(2)}, u32[]{:S(2)}) async-start(f32[3,162,2,512]{1,2,0,3:T(2,128)} %copy.132), calls=%async_computation.1 | async-start | bytes 6291456 | tf_op jit(solution)/shard_map/all_to_all | solution.py:184
  275.5 6.8 %collective-permute-start = (f32[3,8,1,9,256]{4,2,0,1,3:T(1,128)S(1)}, f32[3,8,1,9,256]{4,2,0,1,3:T(1,128)S(1)}, u32[]{:S(2)}, u32[]{:S(2)}) collective-permute-start(f32[3,8,1,9,256]{4,2,0,1,3:T(1,128)S(1)} %get-tuple-element.33), channel_id=1, source_target_pairs={{0,4},{4,8},{8,12},{12,16},{16,20},{20,24},{24,28},{28,0},{1,5},{5... | collective-permute-start | bytes 663560 | tf_op jit(solution)/shard_map/ppermute | solution.py:45
  275.6 6.8 %collective-permute-start.1 = (f32[3,8,1,9,256]{4,2,0,1,3:T(1,128)S(1)}, f32[3,8,1,9,256]{4,2,0,1,3:T(1,128)S(1)}, u32[]{:S(2)}, u32[]{:S(2)}) collective-permute-start(f32[3,8,1,9,256]{4,2,0,1,3:T(1,128)S(1)} %get-tuple-element.34), channel_id=1, source_target_pairs={{4,0},{8,4},{12,8},{16,12},{20,16},{24,20},{28,24},{0,28},{5,1},{9... | collective-permute-start | bytes 663560 | tf_op jit(solution)/shard_map/ppermute | solution.py:46
  278.2 19.9 %copy-start.39 = (f32[256]{0:T(256)}, f32[256]{0:T(256)S(1)}, u32[]{:S(2)}) copy-start(f32[256]{0:T(256)S(1)} %pad_maximum_fusion.6) | copy-start | bytes 3076
  298.1 9.1 %copy-start.36 = (f32[9]{0:T(128)S(1)}, f32[9]{0:T(128)}, u32[]{:S(2)}) copy-start(f32[9]{0:T(128)} %or_select_fusion) | copy-start | bytes 112
  304.3 7.6 %collective-permute-start.2 = (f32[3,8,1,9,256]{4,2,0,1,3:T(1,128)S(1)}, f32[3,8,1,9,256]{4,2,0,1,3:T(1,128)S(1)}, u32[]{:S(2)}, u32[]{:S(2)}) collective-permute-start(f32[3,8,1,9,256]{4,2,0,1,3:T(1,128)S(1)} %get-tuple-element.29), channel_id=1, source_target_pairs={{0,4},{4,8},{8,12},{12,16},{16,20},{20,24},{24,28},{28,0},{1,5},{5... | collective-permute-start | bytes 663560 | tf_op jit(solution)/shard_map/ppermute | solution.py:45
  306.1 5.8 %collective-permute-start.3 = (f32[3,8,1,9,256]{4,2,0,1,3:T(1,128)S(1)}, f32[3,8,1,9,256]{4,2,0,1,3:T(1,128)S(1)}, u32[]{:S(2)}, u32[]{:S(2)}) collective-permute-start(f32[3,8,1,9,256]{4,2,0,1,3:T(1,128)S(1)} %get-tuple-element.30), channel_id=1, source_target_pairs={{4,0},{8,4},{12,8},{16,12},{20,16},{24,20},{28,24},{0,28},{5,1},{9... | collective-permute-start | bytes 663560 | tf_op jit(solution)/shard_map/ppermute | solution.py:46
  337.5 12.5 %copy-start = (f32[3,8,9,9,256]{4,2,3,1,0:T(8,128)}, f32[3,8,9,9,256]{4,2,3,1,0:T(8,128)S(1)}, u32[]{:S(2)}) copy-start(f32[3,8,9,9,256]{4,2,3,1,0:T(8,128)S(1)} %get-tuple-element.25) | copy-start | bytes 5971972
  358.2 21.6 %collective-permute-start.4 = (f32[3,8,1,9,256]{4,2,0,1,3:T(1,128)}, f32[3,8,1,9,256]{4,2,0,1,3:T(1,128)}, u32[]{:S(2)}, u32[]{:S(2)}) collective-permute-start(f32[3,8,1,9,256]{4,2,0,1,3:T(1,128)} %get-tuple-element.23), channel_id=1, source_target_pairs={{0,4},{4,8},{8,12},{12,16},{16,20},{20,24},{24,28},{28,0},{1,5},{5... | collective-permute-start | bytes 663560 | tf_op jit(solution)/shard_map/ppermute | solution.py:45
  358.2 21.6 %collective-permute-start.5 = (f32[3,8,1,9,256]{4,2,0,1,3:T(1,128)}, f32[3,8,1,9,256]{4,2,0,1,3:T(1,128)}, u32[]{:S(2)}, u32[]{:S(2)}) collective-permute-start(f32[3,8,1,9,256]{4,2,0,1,3:T(1,128)} %get-tuple-element.24), channel_id=1, source_target_pairs={{4,0},{8,4},{12,8},{16,12},{20,16},{24,20},{28,24},{0,28},{5,1},{9... | collective-permute-start | bytes 663560 | tf_op jit(solution)/shard_map/ppermute | solution.py:46
  363.8 6.5 %copy-start.24 = (f32[3,256]{1,0:T(4,128)S(1)}, f32[3,256]{1,0:T(4,128)}, u32[]{:S(2)}) copy-start(f32[3,256]{1,0:T(4,128)} %copy-done.23) | copy-start | bytes 9220
  384.3 13.4 %copy-start.26 = (f32[3,256]{1,0:T(4,128)S(1)}, f32[3,256]{1,0:T(4,128)}, u32[]{:S(2)}) copy-start(f32[3,256]{1,0:T(4,128)} %get-tuple-element.11) | copy-start | bytes 9220
  384.3 13.4 %copy-start.27 = (f32[3,256]{1,0:T(4,128)S(1)}, f32[3,256]{1,0:T(4,128)}, u32[]{:S(2)}) copy-start(f32[3,256]{1,0:T(4,128)} %get-tuple-element.12) | copy-start | bytes 9220
  (25 other events, 88.8 us)
where the time goes:
time: 409 us; the launch traced here: 404 us
  matrix products  106 us (26%)
  local copies, waits for them, and re-layouts  84.7 us (21%)
  other arithmetic  79.2 us (19%)
  waiting for transfers between devices  71.7 us (18%)
  blocking collectives  39.5 us (10%)
  starting transfers between devices  19.2 us (5%)
    all_to_all x1, waiting for transfers between devices, on_device(): lax.all_to_all(spectral, 'mode', split_axis=3, concat_axis=1, tiled=True)  63.4 us
    psum x2, blocking collectives, paired(): lax.psum((weighted_sum(residual, residual, multiplicity), weighted_sum(re...  26.7 us
    concatenate x4, local copies, waits for them, and re-layouts, assemble(): jnp.concatenate([jnp.roll(upper_layer, 1, axis=1)[:, :, :, None], nodal_f...  17.2 us
    dot_general x1, matrix products, on_device(): jnp.einsum('peabq,ql->peabl', tendency, forward, precision=highest)  17.1 us
    dot_general x1, matrix products, on_device(): jnp.einsum('ij,pejbq->peibq', derivative, values, precision=highest)  14.2 us
    mul x2, other arithmetic, spectral_tables(): -wave_number * mode_weight * sine_table  14.2 us
    mul x1, other arithmetic, spectral_tables(): -mode_weight * sine_table  14.2 us
    cos x1, other arithmetic, spectral_tables(): cosine_table = jnp.cos(angles)  14 us
  transfers between devices with their start and end apart: 8, of which 3 were waited for; matrix products, arithmetic and copies ran while one was open for 17% of the time, Pallas kernels for 0%

commit v1 on v0

--- a/solution.py
+++ b/solution.py
@@ -33,6 +33,27 @@
 time_step = 0.02
 thrust_coef = 4.0 / 3.0
 highest = lax.Precision.HIGHEST
+
+
+def treat_flows_on(packet):
+    across = "mode"
+    field_out = lax.psum(1, across)
+    outer = lax.axis_index(across)
+    response, w_next = (field_out, outer)
+    latest = list(packet.shape)
+    r2 = packet.shape[3] // response
+    latest[3] = r2
+    moved = latest[1]
+    latest[1] = moved * response
+    current_block = jnp.zeros(latest, packet.dtype)
+    for k0 in range(response):
+        d_next = lax.dynamic_slice_in_dim(packet, (w_next ^ k0) * r2, r2, axis=3)
+        if k0:
+            d_next = lax.ppermute(d_next, across, [(m, m ^ k0) for m in range(response)])
+        current_block = lax.dynamic_update_slice_in_dim(
+            current_block, d_next, (w_next ^ k0) * moved, axis=1
+        )
+    return current_block
 
 
 def padded(shard, sides, width):
@@ -181,7 +202,7 @@
     tendency = jnp.concatenate([(thrust - advection[0])[None], -advection[1:]], axis=0)
     spectral = jnp.einsum("peabq,ql->peabl", tendency, forward, precision=highest)
     spectral = spectral.reshape(3, local_elems * 81, 2, mode_count)
-    returned = lax.all_to_all(spectral, "mode", split_axis=3, concat_axis=1, tiled=True)
+    returned = treat_flows_on(spectral)
     u_star = nodal_field + time_step * returned.reshape(3, elements, 9, 9, 2 * local_modes)
     jacobian = col_width * row_height / 4.0
     ratio_x = row_height / col_width

time: 409 us -> 376 us (0.919)
  the two profiles are of different devices: /device:TPU:0 before, /device:TPU:12 now
where the time goes in v1:
time: 376 us; the launch traced here: 369 us
  matrix products  106 us (28%)
  other arithmetic  85.7 us (23%)
  local copies, waits for them, and re-layouts  72.4 us (19%)
  waiting for transfers between devices  48.9 us (13%)
  blocking collectives  34.5 us (9%)
  starting transfers between devices  18.1 us (5%)
    ppermute x3, waiting for transfers between devices, treat_flows_on(): lax.ppermute(d_next, across, [(m, m ^ k0) for m in range(response)])  38.3 us
    psum x2, blocking collectives, paired(): lax.psum((weighted_sum(residual, residual, multiplicity), weighted_sum(re...  25 us
    dot_general x1, matrix products, on_device(): jnp.einsum('peabq,ql->peabl', tendency, forward, precision=highest)  17.4 us
    concatenate x4, local copies, waits for them, and re-layouts, assemble(): jnp.concatenate([jnp.roll(upper_layer, 1, axis=1)[:, :, :, None], nodal_f...  17.2 us
    mul x2, other arithmetic, spectral_tables(): -wave_number * mode_weight * sine_table  14.1 us
    dot_general x1, matrix products, on_device(): jnp.einsum('ij,pejbq->peibq', derivative, values, precision=highest)  14 us
    cos x1, other arithmetic, spectral_tables(): cosine_table = jnp.cos(angles)  13.9 us
    dot_general x1, matrix products, on_device(): along_z = jnp.einsum('pnl,lq->pnq', flat_items, spanwise, precision=highest)  13.4 us
  transfers between devices with their start and end apart: 10, of which 5 were waited for; matrix products, arithmetic and copies ran while one was open for 21% of the time, Pallas kernels for 0%

profile of v1, /device:TPU:12, one launch (start us, length us, event | category | flops | bytes accessed | tf_op | source)
XLA Modules:
  0.0 369.0 jit_solution(12019043204662519583)
XLA Ops:
  3.6 5.3 %all-to-all-start = ((f32[3,648,2,128]{3,2,0,1:T(2,128)}), f32[3,648,2,128]{3,2,0,1:T(2,128)S(1)}, u32[]{:S(2)}, u32[]{:S(2)}) async-start(f32[3,648,2,128]{3,2,0,1:T(2,128)} %copy.80), calls=%async_computation | async-start | bytes 3981312 | tf_op jit(solution)/shard_map/all_to_all | solution.py:173
  12.3 13.9 %fusion.60 = (f32[512,1536]{1,0:T(8,128)}, f32[512,1536]{1,0:T(8,128)}) fusion(), kind=kLoop, calls=%fused_computation.86 | loop fusion | flops 7864320 | bytes 6291456 | tf_op jit(solution)/shard_map/cos | solution.py:91
  26.3 12.8 %fusion.63 = f32[512,1536]{1,0:T(8,128)} fusion(f32[512]{0:T(512)S(1)} %get-tuple-element.68), kind=kLoop, calls=%fused_computation.89 | loop fusion | flops 7864320 | bytes 3147776 | tf_op jit(solution)/shard_map/mul | solution.py:97
  39.1 12.7 %fusion.71 = f32[512,1536]{1,0:T(8,128)} fusion(f32[512]{0:T(512)S(1)} %get-tuple-element.67), kind=kLoop, calls=%fused_computation.102 | loop fusion | flops 7864320 | bytes 3147776 | tf_op jit(solution)/shard_map/mul | solution.py:97
  51.8 14.1 %fusion.62 = (f32[512,1536]{1,0:T(8,128)}, f32[512,1536]{1,0:T(8,128)}) fusion(f32[512]{0:T(512)S(1)} %negate_multiply_fusion), kind=kLoop, calls=%fused_computation.88 | loop fusion | flops 8650752 | bytes 6293504 | tf_op jit(solution)/shard_map/mul | solution.py:99
  71.3 13.4 %fusion.53 = f32[3,162,1536]{2,1,0:T(8,128)S(1)} fusion(f32[3,162,1024]{2,1,0:T(8,128)} %reshape.200, f32[512,1536]{1,0:T(8,128)S(1)} %copy-done.12, f32[512,1536]{1,0:T(8,128)} %fusion.71), kind=kOutput, calls=%fused_computation.78 | convolution fusion | flops 9174515712 | bytes 11268096 | tf_op jit(solution)/shard_map/pnl,lq->pnq/dot_general | solution.py:175
  102.9 13.4 %fusion.52 = f32[3,162,1536]{2,1,0:T(8,128)S(1)} fusion(f32[3,162,1024]{2,1,0:T(8,128)} %reshape.200, f32[512,1536]{1,0:T(8,128)} %get-tuple-element.60, f32[512,1536]{1,0:T(8,128)S(1)} %copy-done.11), kind=kOutput, calls=%fused_computation.77 | convolution fusion | flops 9174515712 | bytes 11268096 | tf_op jit(solution)/shard_map/pnl,lq->pnq/dot_general | solution.py:176
  120.5 9.5 %psum.35 = f32[]{:T(128)} all-reduce(f32[]{:T(128)} %get-tuple-element.35), channel_id=1, replica_groups=mesh['elem'=8,'mode'=4] {'mode'}, use_global_device_ids=true, to_apply=%region_1.2 | all-reduce | flops 1 | bytes 8 | tf_op jit(solution)/shard_map/psum | solution.py:192
  132.3 11.5 %fusion.16 = f32[3,2,9,1536,9]{3,4,2,1,0:T(8,128)} fusion(f32[9,9,1,1,1]{1,0,4,3,2:T(8,128)S(1)} %copy-done.14, f32[3,2,9,9,1536]{4,0,3,2,1:T(4,128)} %bitcast.133), kind=kOutput, calls=%fused_computation.24 | convolution fusion | flops 80621568 | bytes 5972292 | tf_op jit(solution)/shard_map/ij,peajq->peaiq/dot_general | solution.py:180
  143.8 14.0 %fusion.15 = f32[3,2,9,9,1536]{4,2,3,1,0:T(8,128)S(1)} fusion(f32[3,2,9,9,1536]{4,0,3,2,1:T(4,128)S(1)} %bitcast.135, f32[3,2,9,1536,9]{3,4,2,1,0:T(8,128)} %fusion.16, f32[9,9,1,1,1]{1,0,4,3,2:T(8,128)S(1)} %copy-done.14, f32[3,2,9,9,1536]{4,0,3,2,1:T(4,128)S(1)} %bitcast.134, f32[2,9,9,1536]{3,1,2,0:T(8,128)S(1)} %copy-done.3, f32[2]{0:T(128)S(1)} %copy-done.31, ...), kind=kOutput, calls=%fused_computation.20 | convolution fusion | flops 85847040 | bytes 14930256 | tf_op jit(solution)/shard_map/ij,pejbq->peibq/dot_general | solution.py:179
  160.8 17.4 %fusion.7 = f32[3,2,9,9,1024]{4,2,3,1,0:T(8,128)S(1)} fusion(f32[512,1536]{1,0:T(8,128)S(1)} %copy-done.10, f32[512,1536]{1,0:T(8,128)S(1)} %copy-done.9, f32[2,2,9,9,1536]{4,2,3,1,0:T(8,128)S(1)} %slice_negate_fusion, f32[1,2,9,9,1536]{4,2,3,1,0:T(8,128)S(1)} %slice_subtract_fusion), kind=kOutput, calls=%fused_computation.10 | convolution fusion | flops 9176835072 | bytes 11268096 | tf_op jit(solution)/shard_map/peabq,ql->peabl/dot_general | solution.py:203
  192.5 13.5 %collective-permute-done = f32[3,162,2,128]{3,2,0,1:T(2,128)} collective-permute-done((f32[3,162,2,128]{3,2,0,1:T(2,128)}, f32[3,162,2,128]{3,2,0,1:T(2,128)}, u32[]{:S(2)}, u32[]{:S(2)}) %collective-permute-start) | collective-permute-done | bytes 497696 | tf_op jit(solution)/shard_map/ppermute | solution.py:52
  207.3 16.1 %collective-permute-done.1 = f32[3,162,2,128]{3,2,0,1:T(2,128)S(1)} collective-permute-done((f32[3,162,2,128]{3,2,0,1:T(2,128)S(1)}, f32[3,162,2,128]{3,2,0,1:T(2,128)S(1)}, u32[]{:S(2)}, u32[]{:S(2)}) %collective-permute-start.1) | collective-permute-done | bytes 497696 | tf_op jit(solution)/shard_map/ppermute | solution.py:52
  223.6 8.7 %collective-permute-done.2 = f32[3,162,2,128]{3,2,0,1:T(2,128)S(1)} collective-permute-done((f32[3,162,2,128]{3,2,0,1:T(2,128)S(1)}, f32[3,162,2,128]{3,2,0,1:T(2,128)S(1)}, u32[]{:S(2)}, u32[]{:S(2)}) %collective-permute-start.2) | collective-permute-done | bytes 497696 | tf_op jit(solution)/shard_map/ppermute | solution.py:52
  243.6 4.9 %collective-permute-done.3 = f32[3,8,1,9,256]{4,2,0,1,3:T(1,128)S(1)} collective-permute-done((f32[3,8,1,9,256]{4,2,0,1,3:T(1,128)S(1)}, f32[3,8,1,9,256]{4,2,0,1,3:T(1,128)S(1)}, u32[]{:S(2)}, u32[]{:S(2)}) %collective-permute-start.3) | collective-permute-done | bytes 221216 | tf_op jit(solution)/shard_map/ppermute | solution.py:66
  251.1 4.9 %fusion.45 = f32[3,8,9,256,9]{3,4,2,1,0:T(8,128)S(1)} fusion(f32[9,9,1,1,1]{1,0,4,3,2:T(8,128)S(1)} %copy-done.14, f32[3,8,9,9,256]{4,2,3,1,0:T(8,128)S(1)} %copy_multiply_fusion.5), kind=kOutput, calls=%fused_computation.65 | convolution fusion | flops 53747712 | bytes 3981636 | tf_op jit(solution)/shard_map/ij,peajl->peail/dot_general | solution.py:127
  264.2 6.0 %fusion.32 = f32[3,8,9,9,256]{4,2,0,1,3:T(8,128)S(1)} fusion(f32[3,8,9,256,9]{3,4,2,1,0:T(8,128)S(1)} %fusion.33, f32[8,9,9]{1,0,2:T(8,128)S(1)} %copy-done.23, f32[256]{0:T(256)S(1)} %pad_maximum_fusion.6, f32[3,8,9,1,256]{4,2,0,1,3:T(8,128)S(1)} %maximum_add_fusion.1, f32[3,8,1,9,256]{4,2,0,1,3:T(1,128)S(1)} %get-tuple-element.32, ...), kind=kOutput, calls=%fused_computation.48 | convolution fusion | flops 61212672 | bytes 8408932 | tf_op jit(solution)/shard_map/ji,pejbl->peibl/dot_general | solution.py:130
  273.5 5.7 %collective-permute-done.5 = f32[3,8,1,9,256]{4,2,0,1,3:T(1,128)S(1)} collective-permute-done((f32[3,8,1,9,256]{4,2,0,1,3:T(1,128)S(1)}, f32[3,8,1,9,256]{4,2,0,1,3:T(1,128)S(1)}, u32[]{:S(2)}, u32[]{:S(2)}) %collective-permute-start.5) | collective-permute-done | bytes 221216 | tf_op jit(solution)/shard_map/ppermute | solution.py:66
  283.6 12.9 %all-reduce.1 = (f32[3,256]{1,0:T(4,128)}, f32[3,256]{1,0:T(4,128)}) all-reduce(f32[3,256]{1,0:T(4,128)} %get-tuple-element.8, f32[3,256]{1,0:T(4,128)} %get-tuple-element.7), channel_id=1, replica_groups=mesh['elem'=8,'mode'=4] {'elem'}, use_global_device_ids=true, to_apply=%region_4.5 | all-reduce | flops 1536 | bytes 12288 | tf_op jit(solution)/shard_map/psum | solution.py:144
  297.8 5.0 %multiply_subtract_fusion = (f32[3,8,9,9,256]{4,2,3,1,0:T(8,128)S(1)}, f32[3,8,9,9,256]{4,2,3,1,0:T(8,128)}) fusion(f32[3,256]{1,0:T(4,128)S(1)} %get-tuple-element.14, f32[3,8,9,9,256]{4,2,0,1,3:T(8,128)S(1)} %fusion.25, f32[3,8,9,1,256]{4,2,3,1,0:T(8,128)} %copy-done.8, f32[3,7,9,256]{3,2,0,1:T(8,128)} %copy-done.13, f32[3,1,9,256]{3,2,0,1:T(8,128)} %copy-done.15, ...), kind=kLoop, calls=%fused_computation.71 | loop fusion | flops 2543616 | bytes 7965696 | tf_op jit(solution)/shard_map/sub | solution.py:229
  302.8 4.9 %fusion.42 = f32[3,8,9,256,9]{3,4,2,1,0:T(8,128)S(1)} fusion(f32[9,9,1,1,1]{1,0,4,3,2:T(8,128)S(1)} %copy-done.14, f32[3,8,9,9,256]{4,2,3,1,0:T(8,128)S(1)} %get-tuple-element.25), kind=kOutput, calls=%fused_computation.61 | convolution fusion | flops 53747712 | bytes 3981636 | tf_op jit(solution)/shard_map/ij,peajl->peail/dot_general | solution.py:127
  315.3 5.2 %fusion.27 = f32[3,8,9,9,256]{4,2,0,1,3:T(8,128)S(1)} fusion(f32[3,8,9,256,9]{3,4,2,1,0:T(8,128)S(1)} %fusion.28, f32[3,8,9,9,256]{4,2,3,1,0:T(8,128)S(1)} %get-tuple-element.25, f32[9,9,1,1,1]{1,0,2,3,4:T(8,128)S(1)} %copy-done.30, f32[3,8,9,9,256]{4,2,3,1,0:T(8,128)S(1)} %fusion.30, f32[256]{0:T(256)S(1)} %copy-done.41, f32[8,9,9]{1,0,2:T(8,128)S(1)} %copy-done.16), kind=kOutput, calls=%fused_computation.41 | convolution fusion | flops 56236032 | bytes 7966564 | tf_op jit(solution)/shard_map/ji,pejbl->peibl/dot_general | solution.py:130
  335.5 5.0 %copy.118 = f32[3,8,9,9,256]{4,0,3,2,1:T(4,128)} copy(f32[3,8,9,9,256]{4,2,3,1,0:T(8,128)} %get-tuple-element.26) | data formatting | bytes 3981312 | tf_op jit(solution)/shard_map/concatenate | solution.py:115
  350.9 12.1 %all-reduce = (f32[3,256]{1,0:T(4,128)S(1)}, f32[3,256]{1,0:T(4,128)S(1)}) all-reduce(f32[3,256]{1,0:T(4,128)S(1)} %get-tuple-element.6, f32[3,256]{1,0:T(4,128)S(1)} %get-tuple-element.5), channel_id=1, replica_groups=mesh['elem'=8,'mode'=4] {'elem'}, use_global_device_ids=true, to_apply=%region_8.9 | all-reduce | flops 1536 | bytes 12288 | tf_op jit(solution)/shard_map/psum | solution.py:144
  (193 shorter events, 122.8 us)
Async XLA Ops:
  0.0 9.7 %copy-start.36 = (s32[8]{0:T(128)S(1)}, s32[8]{0:T(128)}, u32[]{:S(2)}) copy-start(s32[8]{0:T(128)} %param.9) | copy-start | bytes 100
  3.6 62.4 %all-to-all-start = ((f32[3,648,2,128]{3,2,0,1:T(2,128)}), f32[3,648,2,128]{3,2,0,1:T(2,128)S(1)}, u32[]{:S(2)}, u32[]{:S(2)}) async-start(f32[3,648,2,128]{3,2,0,1:T(2,128)} %copy.80), calls=%async_computation | async-start | bytes 3981312 | tf_op jit(solution)/shard_map/all_to_all | solution.py:173
  9.7 29.4 %copy-start.17 = (f32[9,9]{1,0:T(8,128)}, f32[9,9]{1,0:T(8,128)S(1)}, u32[]{:S(2)}) copy-start(f32[9,9]{1,0:T(8,128)S(1)} %copy.79) | copy-start | bytes 976
  12.3 76.8 %copy-start.22 = (f32[1536]{0:T(1024)}, f32[1536]{0:T(1024)S(1)}, u32[]{:S(2)}) copy-start(f32[1536]{0:T(1024)S(1)} %fusion.75) | copy-start | bytes 18436
  116.3 16.0 %copy-start.14 = (f32[9,9,1,1,1]{1,0,4,3,2:T(8,128)S(1)}, f32[9,9,1,1,1]{1,0,4,3,2:T(8,128)}, u32[]{:S(2)}) copy-start(f32[9,9,1,1,1]{1,0,4,3,2:T(8,128)} %constant.85) | copy-start | bytes 976
  132.2 11.5 %copy-start.2 = (f32[3,162,1536]{2,0,1:T(4,128)S(1)}, f32[3,162,1536]{2,0,1:T(4,128)}, u32[]{:S(2)}) copy-start(f32[3,162,1536]{2,0,1:T(4,128)} %copy.83) | copy-start | bytes 8957956
  132.2 11.5 %copy-start.3 = (f32[2,9,9,1536]{3,1,2,0:T(8,128)S(1)}, f32[2,9,9,1536]{3,1,2,0:T(8,128)}, u32[]{:S(2)}) copy-start(f32[2,9,9,1536]{3,1,2,0:T(8,128)} %copy.88) | copy-start | bytes 2985988
  132.2 11.5 %copy-start.5 = (f32[3,162,1536]{2,0,1:T(4,128)S(1)}, f32[3,162,1536]{2,0,1:T(4,128)}, u32[]{:S(2)}) copy-start(f32[3,162,1536]{2,0,1:T(4,128)} %copy.89) | copy-start | bytes 8957956
  132.3 11.5 %copy-start.31 = (f32[2]{0:T(128)S(1)}, f32[2]{0:T(128)}, u32[]{:S(2)}) copy-start(f32[2]{0:T(128)} %get-tuple-element.66) | copy-start | bytes 28
  179.5 10.1 %copy-start.37 = (f32[8]{0:T(128)S(1)}, f32[8]{0:T(128)}, u32[]{:S(2)}) copy-start(f32[8]{0:T(128)} %get-tuple-element.63) | copy-start | bytes 100
  185.8 46.7 %copy-start.7 = (f32[3,648,2,128]{3,2,1,0:T(2,128)S(1)}, f32[3,648,2,128]{3,2,1,0:T(2,128)}, u32[]{:S(2)}) copy-start(f32[3,648,2,128]{3,2,1,0:T(2,128)} %param.6) | copy-start | bytes 5971972
  185.8 20.2 %collective-permute-start = (f32[3,162,2,128]{3,2,0,1:T(2,128)}, f32[3,162,2,128]{3,2,0,1:T(2,128)}, u32[]{:S(2)}, u32[]{:S(2)}) collective-permute-start(f32[3,162,2,128]{3,2,0,1:T(2,128)} %get-tuple-element.41), channel_id=1, source_target_pairs={{0,1},{1,0},{2,3},{3,2},{4,5},{5,4},{6,7},{7,6},{8,9},{9,8},{10,11... | collective-permute-start | bytes 1493000 | tf_op jit(solution)/shard_map/ppermute | solution.py:52
  190.3 33.1 %collective-permute-start.1 = (f32[3,162,2,128]{3,2,0,1:T(2,128)S(1)}, f32[3,162,2,128]{3,2,0,1:T(2,128)S(1)}, u32[]{:S(2)}, u32[]{:S(2)}) collective-permute-start(f32[3,162,2,128]{3,2,0,1:T(2,128)S(1)} %get-tuple-element.40), channel_id=1, source_target_pairs={{0,2},{1,3},{2,0},{3,1},{4,6},{5,7},{6,4},{7,5},{8,10},{9,11},{10,... | collective-permute-start | bytes 1493000 | tf_op jit(solution)/shard_map/ppermute | solution.py:52
  190.3 42.0 %collective-permute-start.2 = (f32[3,162,2,128]{3,2,0,1:T(2,128)S(1)}, f32[3,162,2,128]{3,2,0,1:T(2,128)S(1)}, u32[]{:S(2)}, u32[]{:S(2)}) collective-permute-start(f32[3,162,2,128]{3,2,0,1:T(2,128)S(1)} %get-tuple-element.39), channel_id=1, source_target_pairs={{0,3},{1,2},{2,1},{3,0},{4,7},{5,6},{6,5},{7,4},{8,11},{9,10},{10,... | collective-permute-start | bytes 1493000 | tf_op jit(solution)/shard_map/ppermute | solution.py:52
  240.6 7.8 %collective-permute-start.3 = (f32[3,8,1,9,256]{4,2,0,1,3:T(1,128)S(1)}, f32[3,8,1,9,256]{4,2,0,1,3:T(1,128)S(1)}, u32[]{:S(2)}, u32[]{:S(2)}) collective-permute-start(f32[3,8,1,9,256]{4,2,0,1,3:T(1,128)S(1)} %get-tuple-element.33), channel_id=1, source_target_pairs={{0,4},{4,8},{8,12},{12,16},{16,20},{20,24},{24,28},{28,0},{1,5},{5... | collective-permute-start | bytes 663560 | tf_op jit(solution)/shard_map/ppermute | solution.py:66
  240.7 7.8 %collective-permute-start.4 = (f32[3,8,1,9,256]{4,2,0,1,3:T(1,128)S(1)}, f32[3,8,1,9,256]{4,2,0,1,3:T(1,128)S(1)}, u32[]{:S(2)}, u32[]{:S(2)}) collective-permute-start(f32[3,8,1,9,256]{4,2,0,1,3:T(1,128)S(1)} %get-tuple-element.34), channel_id=1, source_target_pairs={{4,0},{8,4},{12,8},{16,12},{20,16},{24,20},{28,24},{0,28},{5,1},{9... | collective-permute-start | bytes 663560 | tf_op jit(solution)/shard_map/ppermute | solution.py:67
  243.3 20.8 %copy-start.40 = (f32[256]{0:T(256)}, f32[256]{0:T(256)S(1)}, u32[]{:S(2)}) copy-start(f32[256]{0:T(256)S(1)} %pad_maximum_fusion.6) | copy-start | bytes 3076
  270.4 8.7 %collective-permute-start.5 = (f32[3,8,1,9,256]{4,2,0,1,3:T(1,128)S(1)}, f32[3,8,1,9,256]{4,2,0,1,3:T(1,128)S(1)}, u32[]{:S(2)}, u32[]{:S(2)}) collective-permute-start(f32[3,8,1,9,256]{4,2,0,1,3:T(1,128)S(1)} %get-tuple-element.29), channel_id=1, source_target_pairs={{0,4},{4,8},{8,12},{12,16},{16,20},{20,24},{24,28},{28,0},{1,5},{5... | collective-permute-start | bytes 663560 | tf_op jit(solution)/shard_map/ppermute | solution.py:66
  270.5 8.6 %collective-permute-start.6 = (f32[3,8,1,9,256]{4,2,0,1,3:T(1,128)S(1)}, f32[3,8,1,9,256]{4,2,0,1,3:T(1,128)S(1)}, u32[]{:S(2)}, u32[]{:S(2)}) collective-permute-start(f32[3,8,1,9,256]{4,2,0,1,3:T(1,128)S(1)} %get-tuple-element.30), channel_id=1, source_target_pairs={{4,0},{8,4},{12,8},{16,12},{20,16},{24,20},{28,24},{0,28},{5,1},{9... | collective-permute-start | bytes 663560 | tf_op jit(solution)/shard_map/ppermute | solution.py:67
  302.8 12.4 %copy-start = (f32[3,8,9,9,256]{4,2,3,1,0:T(8,128)}, f32[3,8,9,9,256]{4,2,3,1,0:T(8,128)S(1)}, u32[]{:S(2)}) copy-start(f32[3,8,9,9,256]{4,2,3,1,0:T(8,128)S(1)} %get-tuple-element.25) | copy-start | bytes 5971972
  323.5 21.5 %collective-permute-start.7 = (f32[3,8,1,9,256]{4,2,0,1,3:T(1,128)}, f32[3,8,1,9,256]{4,2,0,1,3:T(1,128)}, u32[]{:S(2)}, u32[]{:S(2)}) collective-permute-start(f32[3,8,1,9,256]{4,2,0,1,3:T(1,128)} %get-tuple-element.23), channel_id=1, source_target_pairs={{0,4},{4,8},{8,12},{12,16},{16,20},{20,24},{24,28},{28,0},{1,5},{5... | collective-permute-start | bytes 663560 | tf_op jit(solution)/shard_map/ppermute | solution.py:66
  323.5 21.6 %collective-permute-start.8 = (f32[3,8,1,9,256]{4,2,0,1,3:T(1,128)}, f32[3,8,1,9,256]{4,2,0,1,3:T(1,128)}, u32[]{:S(2)}, u32[]{:S(2)}) collective-permute-start(f32[3,8,1,9,256]{4,2,0,1,3:T(1,128)} %get-tuple-element.24), channel_id=1, source_target_pairs={{4,0},{8,4},{12,8},{16,12},{20,16},{24,20},{28,24},{0,28},{5,1},{9... | collective-permute-start | bytes 663560 | tf_op jit(solution)/shard_map/ppermute | solution.py:67
  349.6 13.5 %copy-start.27 = (f32[3,256]{1,0:T(4,128)S(1)}, f32[3,256]{1,0:T(4,128)}, u32[]{:S(2)}) copy-start(f32[3,256]{1,0:T(4,128)} %get-tuple-element.11) | copy-start | bytes 9220
  349.6 13.5 %copy-start.28 = (f32[3,256]{1,0:T(4,128)S(1)}, f32[3,256]{1,0:T(4,128)}, u32[]{:S(2)}) copy-start(f32[3,256]{1,0:T(4,128)} %get-tuple-element.12) | copy-start | bytes 9220
  (29 other events, 120.5 us)
